TPU v7x, 256 devices: a whole 4x4x8 slice. The times are simulated.
256 devices in a mesh: dp: 4 (over y), expert: 64 (over x, z, core).
Axes of the slice: x: 4, y: 4, z: 8, core: 2. Of those that a mesh axis runs over, the one named last changes fastest.
Arguments:
- unit_codes: bfloat16 [128, 256, 1536], P('expert', 'dp'), may hold values from -4 to 4
- block_scales: float32 [128, 12, 256], P('expert', None, 'dp'), may hold values from 0.05 to 2
- pair_list: int32 [2048, 2], replicated, may hold values from 0 to 127, as said below
Outputs:
- left_best: float32 [64, 32, 1536], P('expert', None, 'dp')
- right_best: float32 [64, 32, 1536], P('expert', None, 'dp')
Inputs may be any that keep to these rules, and one draw needn't show every extreme that they name: `pair_list`: row 32 * e + s names as its first expert one of 2 * e to 2 * e + 1, and as its second one of the 2 experts starting at 2 * ((e + o_s) mod n), with n = 64; the offsets o_s are nonzero, distinct over s, include 1, n / 2 and n - 1, and are the same for every e.
All inputs are finite; a program needn't handle non-finite values.
Results may differ from a plain program's by a relative error of at most 0.0017.
Values may be sent and summed in bfloat16 or wider, within the bound.
No kernel may reach another device: no remote copies, remote signals or barrier semaphores. Data moves between devices by JAX's collectives and lax.ppermute only.
A program may use at most 128 MiB of HBM per device.

v0:
```python
import math
import jax
import jax.numpy as jnp
from jax import lax
from jax.sharding import PartitionSpec as P

EPSILON = 1e-06


def body(unit_codes, block_scales, pair_list):
    num_devices = lax.axis_size("expert")
    groups = lax.axis_size("dp")
    my_index = lax.axis_index("expert")
    dp_index = lax.axis_index("dp")
    per_device, row_count, unit_count = unit_codes.shape
    num_blocks = block_scales.shape[1]
    block_len = unit_count // num_blocks
    slice_width = unit_count // groups
    factor = jnp.transpose(block_scales, (0, 2, 1))[:, :, :, None]
    acts = (
        unit_codes.astype(jnp.float32).reshape(per_device, row_count, num_blocks, block_len)
        * factor
    )
    acts = acts.reshape(per_device, row_count, unit_count).astype(jnp.bfloat16)
    slot_count = pair_list.shape[0] // num_devices
    pair_table = pair_list.reshape(num_devices, slot_count, 2)
    my_pairs = lax.dynamic_index_in_dim(pair_table, my_index, 0, keepdims=False)
    left_local = my_pairs[:, 0] % per_device
    right_dev = my_pairs[:, 1] // per_device
    is_asked = pair_table[:, :, 1] // per_device == my_index
    chosen = jnp.sum(jnp.where(is_asked, pair_table[:, :, 1] % per_device, 0), axis=1)
    in_use = jnp.any(is_asked, axis=1)
    chooser = ((chosen[:, None] == jnp.arange(per_device)[None, :]) & in_use[:, None]).astype(
        jnp.bfloat16
    )
    own_full = lax.all_gather(acts, "dp", axis=1, tiled=True)
    flattened = acts.reshape(per_device, -1)
    outbound = jnp.dot(chooser, flattened, preferred_element_type=jnp.float32).astype(jnp.bfloat16)
    received = lax.all_to_all(
        outbound.reshape((num_devices,) + acts.shape[1:]),
        "expert",
        split_axis=0,
        concat_axis=0,
        tiled=True,
    )
    wanted = jnp.take(received, right_dev, axis=0)
    partner = lax.all_to_all(wanted, "dp", split_axis=2, concat_axis=1, tiled=True)
    all_rows = partner.shape[1]
    own_square = (
        jnp.einsum("era,era->ea", own_full, own_full, preferred_element_type=jnp.float32) / all_rows
    )
    inv_own = 1.0 / jnp.sqrt(own_square + EPSILON)
    part_square = (
        jnp.einsum("srb,srb->sb", partner, partner, preferred_element_type=jnp.float32) / all_rows
    )
    inv_part = 1.0 / jnp.sqrt(part_square + EPSILON)

    def single(member):
        expert_pick, partner_block, inv_unit = member
        left_rows = jnp.take(own_full, expert_pick, axis=0)
        gram_block = jnp.einsum(
            "ra,rb->ab", left_rows, partner_block, preferred_element_type=jnp.float32
        )
        correlation = (
            gram_block
            / all_rows
            * jnp.take(inv_own, expert_pick, axis=0)[:, None]
            * inv_unit[None, :]
        )
        return (jnp.max(correlation, axis=1), jnp.max(correlation, axis=0))

    def several(member):
        return jax.vmap(single)(member)

    bundle = math.gcd(slot_count, 4)
    stacked = (
        left_local.reshape(-1, bundle),
        partner.reshape(-1, bundle, all_rows, slice_width),
        inv_part.reshape(-1, bundle, slice_width),
    )
    left_part, right_part = lax.map(several, stacked)
    left_part = left_part.reshape(slot_count, unit_count)
    right_part = right_part.reshape(slot_count, slice_width)
    left_all = lax.pmax(left_part, "dp")
    left_out = lax.dynamic_slice_in_dim(left_all, dp_index * slice_width, slice_width, 1)
    target = (right_dev[:, None] == jnp.arange(num_devices)[None, :]).astype(jnp.float32)
    outgoing = jnp.dot(
        target.T, right_part, precision=lax.Precision.HIGHEST, preferred_element_type=jnp.float32
    )
    returned = lax.all_to_all(outgoing, "expert", split_axis=0, concat_axis=0, tiled=True)
    offsets = pair_table[0, :, 1] // per_device
    source_dev = (my_index - offsets) % num_devices
    right_out = jnp.take(returned, source_dev, axis=0)
    return (left_out[None], right_out[None])


def solution(mesh):
    in_specs = (P("expert", "dp", None), P("expert", None, "dp"), P())
    out_specs = (P("expert", None, "dp"), P("expert", None, "dp"))
    return jax.shard_map(body, mesh=mesh, in_specs=in_specs, out_specs=out_specs, check_vma=False)
```

profile of v0, /device:TPU:2, one launch (start us, length us, event | category | flops | bytes accessed | tf_op | source)
XLA Modules:
  0.0 609.7 jit_solution(17279301070880780680)
XLA Ops:
  11.0 3.7 convolution_convert_fusion
  14.7 7.1 %copy.53 = bf16[8,8,64,1536]{3,2,1,0:T(8,128)(2,1)} copy(bf16[8,8,64,1536]{3,1,2,0:T(8,128)(2,1)S(1)} %bitcast.117) | data formatting | bytes 25165824
  21.8 12.2 %all-to-all-start = ((bf16[64,64,1536]{2,1,0:T(8,128)(2,1)}), bf16[64,64,1536]{2,1,0:T(8,128)(2,1)}, u32[]{:S(2)}, u32[]{:S(2)}) async-start(bf16[64,64,1536]{2,1,0:T(8,128)(2,1)} %bitcast.116), calls=%async_computation | async-start | bytes 25165824 | tf_op jit(solution)/shard_map/all_to_all | solution.py:39
  34.1 274.5 %all-to-all-done = bf16[64,64,1536]{2,1,0:T(8,128)(2,1)} async-done(((bf16[64,64,1536]{2,1,0:T(8,128)(2,1)}), bf16[64,64,1536]{2,1,0:T(8,128)(2,1)}, u32[]{:S(2)}, u32[]{:S(2)}) %all-to-all-start) | async-done | bytes 12582944 | tf_op jit(solution)/shard_map/all_to_all | solution.py:39
  308.6 8.1 %gather_fusion.2 = bf16[32,64,1536]{2,1,0:T(8,128)(2,1)} fusion(bf16[64,64,1536]{2,1,0:T(8,128)(2,1)} %all-to-all-done, s32[1024]{0:T(1024)S(1)} %pad_clamp_fusion.2), kind=kCustom, calls=%fused_computation.2 | custom fusion | bytes 12583040 | tf_op jit(solution)/shard_map/jit(_take)/gather | solution.py:46
  316.7 6.1 broadcast_select_fusion
  322.8 18.4 %copy.29 = bf16[32,64,1536]{1,0,2:T(8,128)(2,1)} copy(bf16[32,64,1536]{2,1,0:T(8,128)(2,1)} %broadcast_select_fusion) | data formatting | bytes 12582912 | tf_op jit(solution)/shard_map/jit(_take)/select_n | solution.py:46
  341.2 12.8 %reshape.286 = bf16[4,2,393216]{2,1,0:T(2,128)(2,1)} reshape(bf16[1536,32,64]{2,1,0:T(8,128)(2,1)} %bitcast.118) | data formatting | bytes 12582912
  354.0 5.3 all-to-all-start.1
  360.2 41.9 %all-gather.2.cloned.1.call-done = bf16[2,256,1536]{2,1,0:T(8,128)(2,1)} async-done(((bf16[2,64,1536]{2,1,0:T(8,128)(2,1)}), bf16[2,256,1536]{2,1,0:T(8,128)(2,1)}) %all-gather.2.cloned.1.call-update) | async-done | bytes 1572880 | tf_op jit(solution)/shard_map/all_gather | solution.py:36
  403.9 40.7 %all-to-all-done.1 = bf16[4,2,393216]{2,1,0:T(2,128)(2,1)} async-done(((bf16[4,2,393216]{2,1,0:T(2,128)(2,1)}), bf16[4,2,393216]{2,1,0:T(2,128)(2,1)}, u32[]{:S(2)}, u32[]{:S(2)}) %all-to-all-start.1) | async-done | bytes 6291488 | tf_op jit(solution)/shard_map/all_to_all | solution.py:47
  444.5 12.6 %reshape.287 = bf16[1536,32,64]{2,1,0:T(8,128)(2,1)} reshape(bf16[4,2,393216]{2,1,0:T(2,128)(2,1)} %all-to-all-done.1) | data formatting | bytes 12582912
  457.2 15.1 %copy.45 = bf16[32,64,4,384]{3,2,1,0:T(4,128)(2,1)} copy(bf16[32,64,4,384]{1,0,3,2:T(8,128)(2,1)} %bitcast.119) | data formatting | bytes 12582912 | tf_op jit(solution)/shard_map/all_to_all | solution.py:47
  472.3 4.3 copy.31
  476.6 2.7 copy-done.1
  481.3 64.2 %while.12 = (s32[]{:T(128)}, f32[8,4,1536]{2,1,0:T(4,128)S(1)}, f32[8,4,384]{2,1,0:T(4,128)S(1)}, s32[8,4]{1,0:T(8,128)S(1)}, bf16[2,256,1536]{2,1,0:T(8,128)(2,...) while((s32[]{:T(128)}, f32[8,4,1536]{2,1,0:T(4,128)S(1)}, ...), condition=%wide.region_5.6_spmd, body=%wide.region_2.5_spmd.sunk | while | flops 1218975232 | bytes 10461917 | solution.py:81
  482.0 2.4 gather_fusion.1
  484.4 4.8 fusion.37
  490.0 2.4 gather_fusion.1
  492.4 4.8 fusion.37
  500.5 4.8 fusion.37
  506.0 2.4 gather_fusion.1
  508.5 4.8 fusion.37
  514.1 2.4 gather_fusion.1
  516.5 4.8 fusion.37
  522.1 2.4 gather_fusion.1
  524.5 4.8 fusion.37
  532.6 4.8 fusion.37
  540.6 4.8 fusion.37
  546.5 5.8 all-to-all-start.2
  553.2 8.4 %all-to-all-done.2 = f32[64,1,384]{2,1,0:T(1,128)S(1)} async-done(((f32[64,1,384]{2,1,0:T(1,128)}), f32[64,1,384]{2,1,0:T(1,128)S(1)}, u32[]{:S(2)}, u32[]{:S(2)}) %all-to-all-start.2) | async-done | bytes 98336 | tf_op jit(solution)/shard_map/all_to_all | solution.py:90
  562.8 38.6 %all-reduce.2.cloned.1.call-done = f32[32,1536]{1,0:T(8,128)} async-done(((f32[32,1536]{1,0:T(8,128)}), f32[32,1536]{1,0:T(8,128)}) %all-reduce.2.cloned.1.call-update) | async-done | bytes 196624 | tf_op jit(solution)/shard_map/pmax | solution.py:84
  (109 shorter events, 26.0 us)
Async XLA Ops:
  10.3 4.4 copy-start.2
  21.8 286.8 %all-to-all-start = ((bf16[64,64,1536]{2,1,0:T(8,128)(2,1)}), bf16[64,64,1536]{2,1,0:T(8,128)(2,1)}, u32[]{:S(2)}, u32[]{:S(2)}) async-start(bf16[64,64,1536]{2,1,0:T(8,128)(2,1)} %bitcast.116), calls=%async_computation | async-start | bytes 25165824 | tf_op jit(solution)/shard_map/all_to_all | solution.py:39
  354.0 90.5 %all-to-all-start.1 = ((bf16[4,2,393216]{2,1,0:T(2,128)(2,1)}), bf16[4,2,393216]{2,1,0:T(2,128)(2,1)}, u32[]{:S(2)}, u32[]{:S(2)}) async-start(bf16[4,2,393216]{2,1,0:T(2,128)(2,1)} %reshape.286), calls=%async_computation.1 | async-start | bytes 12582912 | tf_op jit(solution)/shard_map/all_to_all | solution.py:47
  359.3 42.8 %all-gather.2.cloned.1.call-start = ((), (), s32[]{:S(2)}) async-start(), calls=%async_computation.3 | async-start | bytes 1966080 | tf_op jit(solution)/shard_map/all_gather | solution.py:36
  476.6 2.7 copy-start.1
  479.3 2.0 copy-start
  546.5 15.0 %all-to-all-start.2 = ((f32[64,1,384]{2,1,0:T(1,128)}), f32[64,1,384]{2,1,0:T(1,128)S(1)}, u32[]{:S(2)}, u32[]{:S(2)}) async-start(f32[64,1,384]{2,1,0:T(1,128)} %copy.33), calls=%async_computation.2 | async-start | bytes 196608 | tf_op jit(solution)/shard_map/all_to_all | solution.py:90
  552.3 49.1 %all-reduce.2.cloned.1.call-start = ((), (), s32[]{:S(2)}) async-start(), calls=%async_computation.4 | async-start | bytes 393216 | tf_op jit(solution)/shard_map/pmax | solution.py:84
Sparse Core Ops, SparseCore 0:
  361.9 40.1 all-gather.1
  555.5 45.8 all-reduce.1
where the time goes:
time: 611 us; the launch traced here: 610 us
  waiting for transfers between devices  405 us (66%)
  local copies, waits for them, and re-layouts  112 us (18%)
  matrix products  42.6 us (7%)
  starting transfers between devices  23.5 us (4%)
  between operations  14.3 us (2%)
  other arithmetic  12.7 us (2%)
    all_to_all x1, waiting for transfers between devices, body(): lax.all_to_all(outbound.reshape((num_devices,) + acts.shape[1:]), 'expert...  274 us
    all_gather x1, waiting for transfers between devices, body(): own_full = lax.all_gather(acts, 'dp', axis=1, tiled=True)  41.9 us
    all_to_all x1, waiting for transfers between devices, body(): lax.all_to_all(wanted, 'dp', split_axis=2, concat_axis=1, tiled=True)  40.7 us
    dot_general x8, matrix products, single(): jnp.einsum('ra,rb->ab', left_rows, partner_block, preferred_element_type=...  38.6 us
    pmax x1, waiting for transfers between devices, body(): left_all = lax.pmax(left_part, 'dp')  38.6 us
    unnamed x11, local copies, waits for them, and re-layouts  35.6 us
    gather x8, local copies, waits for them, and re-layouts, single(): left_rows = jnp.take(own_full, expert_pick, axis=0)  19.6 us
    all_to_all x2, local copies, waits for them, and re-layouts, body(): lax.all_to_all(wanted, 'dp', split_axis=2, concat_axis=1, tiled=True)  19.4 us
  transfers between devices with their start and end apart: 5, of which 5 were waited for; matrix products, arithmetic and copies ran while one was open for 1% of the time, Pallas kernels for 0%

commit v1 on v0

--- a/solution.py
+++ b/solution.py
@@ -5,6 +5,12 @@
 from jax.sharding import PartitionSpec as P
 
 EPSILON = 1e-06
+
+
+def exchange_blocks(array, mesh_axis, split, join):
+    cells = jnp.split(array, lax.axis_size(mesh_axis), axis=split)
+    arrived = lax.all_to_all(jnp.stack(cells), mesh_axis, 0, 0)
+    return jnp.concatenate(arrived, axis=join)
 
 
 def body(unit_codes, block_scales, pair_list):
@@ -44,7 +50,7 @@
         tiled=True,
     )
     wanted = jnp.take(received, right_dev, axis=0)
-    partner = lax.all_to_all(wanted, "dp", split_axis=2, concat_axis=1, tiled=True)
+    partner = exchange_blocks(wanted, "dp", 2, 1)
     all_rows = partner.shape[1]
     own_square = (
         jnp.einsum("era,era->ea", own_full, own_full, preferred_element_type=jnp.float32) / all_rows

time: 611 us -> 553 us (0.905)
  local copies, waits for them, and re-layouts: 112 us -> 53.2 us
    unnamed x11 -> x9, local copies, waits for them, and re-layouts: 35.6 us -> 10.2 us
    select_n x1 -> x0, local copies, waits for them, and re-layouts: 18.4 us -> none  [body(): wanted = jnp.take(received, right_dev, axis=0)]
    all_to_all x2 -> x1, local copies, waits for them, and re-layouts: 19.4 us -> 3.59 us  [exchange_blocks(): arrived = lax.all_to_all(jnp.stack(cells), mesh_axis, 0, 0)]
where the time goes in v1:
time: 553 us; the launch traced here: 552 us
  waiting for transfers between devices  405 us (73%)
  local copies, waits for them, and re-layouts  53.2 us (10%)
  matrix products  42.6 us (8%)
  starting transfers between devices  23.5 us (4%)
  between operations  14.3 us (3%)
  other arithmetic  13.6 us (2%)
    all_to_all x1, waiting for transfers between devices, body(): lax.all_to_all(outbound.reshape((num_devices,) + acts.shape[1:]), 'expert...  274 us
    all_gather x1, waiting for transfers between devices, body(): own_full = lax.all_gather(acts, 'dp', axis=1, tiled=True)  41.9 us
    all_to_all x1, waiting for transfers between devices, exchange_blocks(): arrived = lax.all_to_all(jnp.stack(cells), mesh_axis, 0, 0)  40.7 us
    dot_general x8, matrix products, single(): jnp.einsum('ra,rb->ab', left_rows, partner_block, preferred_element_type=...  38.6 us
    pmax x1, waiting for transfers between devices, body(): left_all = lax.pmax(left_part, 'dp')  38.6 us
    gather x8, local copies, waits for them, and re-layouts, single(): left_rows = jnp.take(own_full, expert_pick, axis=0)  19.6 us
    all_to_all x1, starting transfers between devices, body(): lax.all_to_all(outbound.reshape((num_devices,) + acts.shape[1:]), 'expert...  12.2 us
  transfers between devices with their start and end apart: 5, of which 5 were waited for; matrix products, arithmetic and copies ran while one was open for 1% of the time, Pallas kernels for 0%

profile of v1, /device:TPU:2, one launch (start us, length us, event | category | flops | bytes accessed | tf_op | source)
XLA Modules:
  0.0 552.1 jit_solution(15554598813296755916)
XLA Ops:
  11.0 3.7 convolution_convert_fusion
  14.7 7.1 %copy.34 = bf16[8,8,64,1536]{3,2,1,0:T(8,128)(2,1)} copy(bf16[8,8,64,1536]{3,1,2,0:T(8,128)(2,1)S(1)} %bitcast.121) | data formatting | bytes 25165824
  21.8 12.2 %all-to-all-start = ((bf16[64,64,1536]{2,1,0:T(8,128)(2,1)}), bf16[64,64,1536]{2,1,0:T(8,128)(2,1)}, u32[]{:S(2)}, u32[]{:S(2)}) async-start(bf16[64,64,1536]{2,1,0:T(8,128)(2,1)} %bitcast.120), calls=%async_computation | async-start | bytes 25165824 | tf_op jit(solution)/shard_map/all_to_all | solution.py:45
  34.1 274.5 %all-to-all-done = bf16[64,64,1536]{2,1,0:T(8,128)(2,1)} async-done(((bf16[64,64,1536]{2,1,0:T(8,128)(2,1)}), bf16[64,64,1536]{2,1,0:T(8,128)(2,1)}, u32[]{:S(2)}, u32[]{:S(2)}) %all-to-all-start) | async-done | bytes 12582944 | tf_op jit(solution)/shard_map/all_to_all | solution.py:45
  308.6 8.1 %gather_fusion.2 = bf16[32,64,1536]{2,1,0:T(8,128)(2,1)} fusion(bf16[64,64,1536]{2,1,0:T(8,128)(2,1)} %all-to-all-done, s32[1024]{0:T(1024)S(1)} %pad_clamp_fusion.2), kind=kCustom, calls=%fused_computation.2 | custom fusion | bytes 12583040 | tf_op jit(solution)/shard_map/jit(_take)/gather | solution.py:52
  316.7 3.4 broadcast_select_fusion
  321.4 3.5 pad_maximum_fusion
  324.9 5.2 all-to-all-start.1
  331.1 41.9 %all-gather.2.cloned.1.call-done = bf16[2,256,1536]{2,1,0:T(8,128)(2,1)} async-done(((bf16[2,64,1536]{2,1,0:T(8,128)(2,1)}), bf16[2,256,1536]{2,1,0:T(8,128)(2,1)}) %all-gather.2.cloned.1.call-update) | async-done | bytes 1572880 | tf_op jit(solution)/shard_map/all_gather | solution.py:42
  374.7 40.7 %all-to-all-done.1 = bf16[4,32,64,384]{3,2,1,0:T(8,128)(2,1)} async-done(((bf16[4,32,64,384]{3,2,1,0:T(8,128)(2,1)}), bf16[4,32,64,384]{3,2,1,0:T(8,128)(2,1)}, u32[]{:S(2)}, u32[]{:S(2)}) %all-to-all-start.1) | async-done | bytes 6291488 | tf_op jit(solution)/shard_map/all_to_all | solution.py:12
  415.4 3.6 copy.17
  419.0 2.7 copy-done.1
  423.7 64.2 %while.12 = (s32[]{:T(128)}, f32[8,4,1536]{2,1,0:T(4,128)S(1)}, f32[8,4,384]{2,1,0:T(4,128)S(1)}, s32[8,4]{1,0:T(8,128)S(1)}, bf16[2,256,1536]{2,1,0:T(8,128)(2,...) while((s32[]{:T(128)}, f32[8,4,1536]{2,1,0:T(4,128)S(1)}, ...), condition=%wide.region_5.6_spmd, body=%wide.region_2.5_spmd.sunk | while | flops 1218975232 | bytes 10461917 | solution.py:87
  424.4 2.4 gather_fusion.1
  426.8 4.8 fusion.37
  432.4 2.4 gather_fusion.1
  434.8 4.8 fusion.37
  440.4 2.4 gather_fusion.1
  442.9 4.8 fusion.37
  448.4 2.4 gather_fusion.1
  450.9 4.8 fusion.37
  456.5 2.4 gather_fusion.1
  458.9 4.8 fusion.37
  464.5 2.4 gather_fusion.1
  466.9 4.8 fusion.37
  472.5 2.4 gather_fusion.1
  475.0 4.8 fusion.37
  480.5 2.4 gather_fusion.1
  483.0 4.8 fusion.37
  488.9 5.8 %all-to-all-start.2 = ((f32[64,1,384]{2,1,0:T(1,128)}), f32[64,1,384]{2,1,0:T(1,128)S(1)}, u32[]{:S(2)}, u32[]{:S(2)}) async-start(f32[64,1,384]{2,1,0:T(1,128)} %copy.18), calls=%async_computation.2 | async-start | bytes 196608 | tf_op jit(solution)/shard_map/all_to_all | solution.py:96
  495.5 8.4 %all-to-all-done.2 = f32[64,1,384]{2,1,0:T(1,128)S(1)} async-done(((f32[64,1,384]{2,1,0:T(1,128)}), f32[64,1,384]{2,1,0:T(1,128)S(1)}, u32[]{:S(2)}, u32[]{:S(2)}) %all-to-all-start.2) | async-done | bytes 98336 | tf_op jit(solution)/shard_map/all_to_all | solution.py:96
  505.2 38.6 %all-reduce.2.cloned.1.call-done = f32[32,1536]{1,0:T(8,128)} async-done(((f32[32,1536]{1,0:T(8,128)}), f32[32,1536]{1,0:T(8,128)}) %all-reduce.2.cloned.1.call-update) | async-done | bytes 196624 | tf_op jit(solution)/shard_map/pmax | solution.py:90
  (107 shorter events, 19.9 us)
Async XLA Ops:
  10.3 4.4 copy-start.2
  21.8 286.8 %all-to-all-start = ((bf16[64,64,1536]{2,1,0:T(8,128)(2,1)}), bf16[64,64,1536]{2,1,0:T(8,128)(2,1)}, u32[]{:S(2)}, u32[]{:S(2)}) async-start(bf16[64,64,1536]{2,1,0:T(8,128)(2,1)} %bitcast.120), calls=%async_computation | async-start | bytes 25165824 | tf_op jit(solution)/shard_map/all_to_all | solution.py:45
  324.9 90.5 %all-to-all-start.1 = ((bf16[4,32,64,384]{3,2,1,0:T(8,128)(2,1)}), bf16[4,32,64,384]{3,2,1,0:T(8,128)(2,1)}, u32[]{:S(2)}, u32[]{:S(2)}) async-start(bf16[4,32,64,384]{3,2,1,0:T(8,128)(2,1)} %pad_maximum_fusion), calls=%async_computation.1 | async-start | bytes 12582912 | tf_op jit(solution)/shard_map/all_to_all | solution.py:12
  330.2 42.8 %all-gather.2.cloned.1.call-start = ((), (), s32[]{:S(2)}) async-start(), calls=%async_computation.3 | async-start | bytes 1966080 | tf_op jit(solution)/shard_map/all_gather | solution.py:42
  419.0 2.7 copy-start.1
  421.7 2.0 copy-start
  488.9 15.0 %all-to-all-start.2 = ((f32[64,1,384]{2,1,0:T(1,128)}), f32[64,1,384]{2,1,0:T(1,128)S(1)}, u32[]{:S(2)}, u32[]{:S(2)}) async-start(f32[64,1,384]{2,1,0:T(1,128)} %copy.18), calls=%async_computation.2 | async-start | bytes 196608 | tf_op jit(solution)/shard_map/all_to_all | solution.py:96
  494.7 49.1 %all-reduce.2.cloned.1.call-start = ((), (), s32[]{:S(2)}) async-start(), calls=%async_computation.4 | async-start | bytes 393216 | tf_op jit(solution)/shard_map/pmax | solution.py:90
Sparse Core Ops, SparseCore 0:
  332.8 40.1 all-gather.1
  497.9 45.8 all-reduce.1
